TPU v7x, 128 devices: a whole 4x4x4 slice. The times are simulated.
128 devices in a mesh: dp: 8 (over x, core), feat: 16 (over z, y).
Axes of the slice: x: 4, y: 4, z: 4, core: 2. Of those that a mesh axis runs over, the one named last changes fastest.
Arguments:
- features: bfloat16 [12288, 65536], P('dp', 'feat'), may hold values from -64 to 64
- weight: float32 [16, 65536], P(None, 'feat'), may hold values from -1 to 1
- labels: int32 [12288], P('dp'), may hold values from 0 to 15
- sample_weight: int32 [12288], P('dp'), may hold values from 1 to 4
Outputs:
- logit_step: float32 [12288, 16], P('dp')
- mean_loss: float32 [], replicated
All inputs are finite; a program needn't handle non-finite values.
Results may differ from a plain program's by a relative error of at most 0.014.
Values may be sent and summed in bfloat16 or wider, within the bound.
A program may use at most 64 MiB of HBM per device.

v0:
```python
import jax
import jax.numpy as jnp
from jax import lax
from jax.sharding import PartitionSpec as P

CG_ITERS = 4


RIDGE_COEF = 0.1
NORM_GUARD = 1e-06


def row_products(features, matrix_b):
    return lax.dot_general(
        features, matrix_b, (((1,), (1,)), ((), ())), preferred_element_type=jnp.float32
    )


def column_products(rows_b, features):
    return lax.dot_general(
        rows_b, features, (((0,), (0,)), ((), ())), preferred_element_type=jnp.float32
    )


def on_device(features, weight, labels, sample_weight):
    classes = weight.shape[0]
    weight_b = weight.astype(jnp.bfloat16)
    logits = lax.psum(row_products(features, weight_b), "feat")
    row_top = jnp.max(logits, axis=1, keepdims=True)
    shifted = jnp.exp(logits - row_top)
    summed = jnp.sum(shifted, axis=1, keepdims=True)
    class_prob = shifted / summed
    log_total = row_top[:, 0] + jnp.log(summed[:, 0])
    row_weight = sample_weight.astype(jnp.float32)
    onehot = (labels[:, None] == jnp.arange(classes, dtype=jnp.int32)[None, :]).astype(jnp.float32)
    picked = jnp.sum(logits * onehot, axis=1)
    weight_total, loss_total = lax.psum(
        (jnp.sum(row_weight), jnp.sum(row_weight * (log_total - picked))), "dp"
    )
    mean_loss = loss_total / weight_total
    row_scale = (row_weight / weight_total)[:, None]
    resid_rows = (row_scale * (class_prob - onehot)).astype(jnp.bfloat16)
    grad_partial = column_products(resid_rows, features)

    def inner_total(value):
        return lax.psum(value, "feat")

    gradient = (
        lax.psum(grad_partial.astype(jnp.bfloat16), "dp").astype(jnp.float32) + RIDGE_COEF * weight
    )
    newton_step = jnp.zeros_like(gradient)
    residual = -gradient
    direction = residual
    res_norm = inner_total(jnp.sum(residual * residual))
    for _ in range(CG_ITERS):
        direction_b = direction.astype(jnp.bfloat16)
        dir_scores = lax.psum(
            row_products(features, direction_b).astype(jnp.bfloat16), "feat"
        ).astype(jnp.float32)
        mixed_mean = jnp.sum(class_prob * dir_scores, axis=1, keepdims=True)
        curv_rows = (row_scale * class_prob * (dir_scores - mixed_mean)).astype(jnp.bfloat16)
        hess_image = (
            lax.psum(column_products(curv_rows, features).astype(jnp.bfloat16), "dp").astype(
                jnp.float32
            )
            + RIDGE_COEF * direction
        )
        step_size = res_norm / inner_total(jnp.sum(direction * hess_image))
        newton_step = newton_step + step_size * direction
        residual = residual - step_size * hess_image
        new_norm = inner_total(jnp.sum(residual * residual))
        direction = residual + new_norm / (res_norm + NORM_GUARD) * direction
        res_norm = new_norm
    step_b = newton_step.astype(jnp.bfloat16)
    logit_step = lax.psum(row_products(features, step_b).astype(jnp.bfloat16), "feat").astype(
        jnp.float32
    )
    return (logit_step, mean_loss)


def solution(mesh):
    in_specs = (P("dp", "feat"), P(None, "feat"), P("dp"), P("dp"))
    out_specs = (P("dp", None), P())
    return jax.shard_map(
        on_device, mesh=mesh, in_specs=in_specs, out_specs=out_specs, check_vma=False
    )
```

profile of v0, /device:TPU:0, one launch (start us, length us, event | category | flops | bytes accessed | tf_op | source)
XLA Modules:
  0.0 1117.8 jit_solution(13051484265639094176)
XLA Ops:
  7.2 0.0 copy-start.5
  7.2 0.0 copy-start.6
  7.2 0.0 all-reduce.8.cloned.1.call-start
  7.2 1.3 convert_reduce_fusion
  8.5 8.6 fusion.12
  17.1 0.0 all-reduce.8.cloned.1.call-update
  17.1 0.0 all-reduce.10.cloned.1.call-start
  17.2 15.4 %psum.147 = f32[]{:T(128)} all-reduce(f32[]{:T(128)} %convert_reduce_fusion), channel_id=1, replica_groups=mesh['dp'=8,'feat'=16] {'dp'}, use_global_device_ids=true, to_apply=%region_1.0 | all-reduce | flops 1 | bytes 8 | tf_op jit(solution)/shard_map/psum | solution.py:37
  32.5 0.0 copy-done.5
  32.5 0.6 convert_divide_fusion
  33.2 69.7 %all-reduce.8.cloned.1.call-done = f32[1536,16]{0,1:T(8,128)} async-done(((f32[1536,16]{0,1:T(8,128)}), f32[1536,16]{0,1:T(8,128)}) %all-reduce.8.cloned.1.call-update) | async-done | bytes 98320 | tf_op jit(solution)/shard_map/psum | solution.py:28
  102.9 0.9 reduce_max.9
  103.8 0.9 fusion.27
  104.8 0.0 copy-done.6
  104.8 0.0 copy-start
  104.8 7.1 convolution_convert_fusion.4
  111.9 0.0 all-reduce.10.cloned.1.call-update
  111.9 0.0 all-reduce.12.cloned.1.call-start
  111.9 58.6 %all-reduce.10.cloned.1.call-done = bf16[16,4096]{1,0:T(8,128)(2,1)} async-done(((bf16[16,4096]{1,0:T(8,128)(2,1)}), bf16[16,4096]{1,0:T(8,128)(2,1)}) %all-reduce.10.cloned.1.call-update) | async-done | bytes 131088 | tf_op jit(solution)/shard_map/psum | solution.py:49
  170.5 0.9 multiply_add_fusion.6
  171.5 7.9 fusion
  179.4 74.6 %psum.151 = bf16[1536,16]{0,1:T(8,128)(2,1)S(1)} all-reduce(bf16[1536,16]{0,1:T(8,128)(2,1)S(1)} %fusion), channel_id=1, replica_groups=mesh['dp'=8,'feat'=16] {'feat'}, use_global_device_ids=true, to_apply=%region_8.0 | all-reduce | flops 24576 | bytes 98304 | tf_op jit(solution)/shard_map/psum | solution.py:57
  254.0 0.1 select_reduce_fusion
  254.1 7.0 convolution_convert_fusion.3
  261.1 0.0 all-reduce.12.cloned.1.call-update
  261.1 0.0 all-reduce.14.cloned.1.call-start
  261.1 53.6 %all-reduce.12.cloned.1.call-done = bf16[16,4096]{1,0:T(8,128)(2,1)} async-done(((bf16[16,4096]{1,0:T(8,128)(2,1)}), bf16[16,4096]{1,0:T(8,128)(2,1)}) %all-reduce.12.cloned.1.call-update) | async-done | bytes 131088 | tf_op jit(solution)/shard_map/psum | solution.py:63
  314.7 1.6 multiply_reduce_fusion.6
  316.3 41.3 %all-reduce = (f32[]{:T(128)}, f32[]{:T(128)}) all-reduce(f32[]{:T(128)} %get-tuple-element.3, f32[]{:T(128)} %get-tuple-element.2), channel_id=1, replica_groups=mesh['dp'=8,'feat'=16] {'feat'}, use_global_device_ids=true, to_apply=%region_7.0 | all-reduce | flops 2 | bytes 16 | tf_op jit(solution)/shard_map/psum | solution.py:46
  359.0 1.6 multiply_reduce_fusion.5
  361.2 36.3 %psum.154 = f32[]{:T(128)} all-reduce(f32[]{:T(128)} %multiply_reduce_fusion.5), channel_id=1, replica_groups=mesh['dp'=8,'feat'=16] {'feat'}, use_global_device_ids=true, to_apply=%region_14.0 | all-reduce | flops 1 | bytes 8 | tf_op jit(solution)/shard_map/psum | solution.py:46
  398.2 8.0 fusion.1
  406.2 71.7 %psum.155 = bf16[1536,16]{0,1:T(8,128)(2,1)S(1)} all-reduce(bf16[1536,16]{0,1:T(8,128)(2,1)S(1)} %fusion.1), channel_id=1, replica_groups=mesh['dp'=8,'feat'=16] {'feat'}, use_global_device_ids=true, to_apply=%region_15.0 | all-reduce | flops 24576 | bytes 98304 | tf_op jit(solution)/shard_map/psum | solution.py:57
  477.9 7.0 convolution_convert_fusion.2
  484.9 0.0 all-reduce.14.cloned.1.call-update
  484.9 0.0 all-reduce.16.cloned.1.call-start
  484.9 53.6 %all-reduce.14.cloned.1.call-done = bf16[16,4096]{1,0:T(8,128)(2,1)} async-done(((bf16[16,4096]{1,0:T(8,128)(2,1)}), bf16[16,4096]{1,0:T(8,128)(2,1)}) %all-reduce.14.cloned.1.call-update) | async-done | bytes 131088 | tf_op jit(solution)/shard_map/psum | solution.py:63
  538.5 0.0 copy-done.1
  538.5 1.7 multiply_reduce_fusion.4
  540.2 41.3 %psum.157 = f32[]{:T(128)} all-reduce(f32[]{:T(128)} %multiply_reduce_fusion.4), channel_id=1, replica_groups=mesh['dp'=8,'feat'=16] {'feat'}, use_global_device_ids=true, to_apply=%region_19.0 | all-reduce | flops 1 | bytes 8 | tf_op jit(solution)/shard_map/psum | solution.py:46
  582.9 1.7 multiply_reduce_fusion.3
  585.2 36.0 %psum.158 = f32[]{:T(128)} all-reduce(f32[]{:T(128)} %multiply_reduce_fusion.3), channel_id=1, replica_groups=mesh['dp'=8,'feat'=16] {'feat'}, use_global_device_ids=true, to_apply=%region_21.0 | all-reduce | flops 1 | bytes 8 | tf_op jit(solution)/shard_map/psum | solution.py:46
  621.9 8.0 fusion.2
  629.9 71.7 %psum.159 = bf16[1536,16]{0,1:T(8,128)(2,1)S(1)} all-reduce(bf16[1536,16]{0,1:T(8,128)(2,1)S(1)} %fusion.2), channel_id=1, replica_groups=mesh['dp'=8,'feat'=16] {'feat'}, use_global_device_ids=true, to_apply=%region_22.0 | all-reduce | flops 24576 | bytes 98304 | tf_op jit(solution)/shard_map/psum | solution.py:57
  701.6 7.0 convolution_convert_fusion.1
  708.6 0.0 all-reduce.16.cloned.1.call-update
  708.6 0.0 all-reduce.18.cloned.1.call-start
  708.6 53.6 %all-reduce.16.cloned.1.call-done = bf16[16,4096]{1,0:T(8,128)(2,1)} async-done(((bf16[16,4096]{1,0:T(8,128)(2,1)}), bf16[16,4096]{1,0:T(8,128)(2,1)}) %all-reduce.16.cloned.1.call-update) | async-done | bytes 131088 | tf_op jit(solution)/shard_map/psum | solution.py:63
  762.3 1.7 multiply_reduce_fusion.2
  763.9 41.2 %psum.161 = f32[]{:T(128)} all-reduce(f32[]{:T(128)} %multiply_reduce_fusion.2), channel_id=1, replica_groups=mesh['dp'=8,'feat'=16] {'feat'}, use_global_device_ids=true, to_apply=%region_26.0 | all-reduce | flops 1 | bytes 8 | tf_op jit(solution)/shard_map/psum | solution.py:46
  806.4 1.7 multiply_reduce_fusion.1
  808.7 36.2 %psum.162 = f32[]{:T(128)} all-reduce(f32[]{:T(128)} %multiply_reduce_fusion.1), channel_id=1, replica_groups=mesh['dp'=8,'feat'=16] {'feat'}, use_global_device_ids=true, to_apply=%region_28.0 | all-reduce | flops 1 | bytes 8 | tf_op jit(solution)/shard_map/psum | solution.py:46
  845.6 8.0 fusion.3
  853.6 71.7 %psum.163 = bf16[1536,16]{0,1:T(8,128)(2,1)S(1)} all-reduce(bf16[1536,16]{0,1:T(8,128)(2,1)S(1)} %fusion.3), channel_id=1, replica_groups=mesh['dp'=8,'feat'=16] {'feat'}, use_global_device_ids=true, to_apply=%region_29.0 | all-reduce | flops 24576 | bytes 98304 | tf_op jit(solution)/shard_map/psum | solution.py:57
  925.3 7.0 convolution_convert_fusion
  932.3 0.0 all-reduce.18.cloned.1.call-update
  932.3 0.7 multiply_reduce_fusion.8
  933.0 13.1 %psum.167 = f32[]{:T(128)} all-reduce(f32[]{:T(128)} %multiply_reduce_fusion.8), channel_id=1, replica_groups=mesh['dp'=8,'feat'=16] {'dp'}, use_global_device_ids=true, to_apply=%region_37.0 | all-reduce | flops 1 | bytes 8 | tf_op jit(solution)/shard_map/psum | solution.py:37
  946.1 39.8 %all-reduce.18.cloned.1.call-done = bf16[16,4096]{1,0:T(8,128)(2,1)} async-done(((bf16[16,4096]{1,0:T(8,128)(2,1)}), bf16[16,4096]{1,0:T(8,128)(2,1)}) %all-reduce.18.cloned.1.call-update) | async-done | bytes 131088 | tf_op jit(solution)/shard_map/psum | solution.py:63
  985.9 1.8 multiply_reduce_fusion
  989.1 41.2 %psum.165 = f32[]{:T(128)} all-reduce(f32[]{:T(128)} %multiply_reduce_fusion), channel_id=1, replica_groups=mesh['dp'=8,'feat'=16] {'feat'}, use_global_device_ids=true, to_apply=%region_33.0 | all-reduce | flops 1 | bytes 8 | tf_op jit(solution)/shard_map/psum | solution.py:46
  1031.6 7.9 fusion.4
  1039.5 69.6 %psum.166 = bf16[1536,16]{0,1:T(8,128)(2,1)S(1)} all-reduce(bf16[1536,16]{0,1:T(8,128)(2,1)S(1)} %fusion.4), channel_id=1, replica_groups=mesh['dp'=8,'feat'=16] {'feat'}, use_global_device_ids=true, to_apply=%region_34.0 | all-reduce | flops 24576 | bytes 98304 | tf_op jit(solution)/shard_map/psum | solution.py:75
  1109.2 0.7 convert_element_type.151
  (11 shorter events, 0.1 us)
Async XLA Ops:
  7.2 25.4 %copy-start.5 = (s32[1536]{0:T(1024)S(1)}, s32[1536]{0:T(1024)}, u32[]{:S(2)}) copy-start(s32[1536]{0:T(1024)} %param.7) | copy-start | bytes 18436
  7.2 97.6 %copy-start.6 = (s32[1536]{0:T(1024)S(1)}, s32[1536]{0:T(1024)}, u32[]{:S(2)}) copy-start(s32[1536]{0:T(1024)} %param.6) | copy-start | bytes 18436
  7.2 95.7 %all-reduce.8.cloned.1.call-start = ((), (), s32[]{:S(2)}) async-start(), calls=%async_computation | async-start | bytes 196608 | tf_op jit(solution)/shard_map/psum | solution.py:28
  17.1 153.4 %copy-start.4 = (f32[16,4096]{1,0:T(8,128)S(1)}, f32[16,4096]{1,0:T(8,128)}, u32[]{:S(2)}) copy-start(f32[16,4096]{1,0:T(8,128)} %param.5) | copy-start | bytes 786436
  17.1 153.4 %all-reduce.10.cloned.1.call-start = ((), (), s32[]{:S(2)}) async-start(), calls=%async_computation.1 | async-start | bytes 262144 | tf_op jit(solution)/shard_map/psum | solution.py:49
  104.8 149.2 %copy-start = (f32[1536,16]{0,1:T(8,128)S(1)}, f32[1536,16]{0,1:T(8,128)}, u32[]{:S(2)}) copy-start(f32[1536,16]{0,1:T(8,128)} %all-reduce.8.cloned.1.call-done) | copy-start | bytes 294916
  111.9 202.9 %all-reduce.12.cloned.1.call-start = ((), (), s32[]{:S(2)}) async-start(), calls=%async_computation.2 | async-start | bytes 262144 | tf_op jit(solution)/shard_map/psum | solution.py:63
  261.1 277.4 %all-reduce.14.cloned.1.call-start = ((), (), s32[]{:S(2)}) async-start(), calls=%async_computation.3 | async-start | bytes 262144 | tf_op jit(solution)/shard_map/psum | solution.py:63
  406.2 132.3 %copy-start.1 = (bf16[16,4096]{1,0:T(8,128)(2,1)S(1)}, bf16[16,4096]{1,0:T(8,128)(2,1)}, u32[]{:S(2)}) copy-start(bf16[16,4096]{1,0:T(8,128)(2,1)} %all-reduce.12.cloned.1.call-done) | copy-start | bytes 393220
  484.9 277.4 %all-reduce.16.cloned.1.call-start = ((), (), s32[]{:S(2)}) async-start(), calls=%async_computation.4 | async-start | bytes 262144 | tf_op jit(solution)/shard_map/psum | solution.py:63
  629.9 132.4 %copy-start.2 = (bf16[16,4096]{1,0:T(8,128)(2,1)S(1)}, bf16[16,4096]{1,0:T(8,128)(2,1)}, u32[]{:S(2)}) copy-start(bf16[16,4096]{1,0:T(8,128)(2,1)} %all-reduce.14.cloned.1.call-done) | copy-start | bytes 393220
  708.6 277.3 %all-reduce.18.cloned.1.call-start = ((), (), s32[]{:S(2)}) async-start(), calls=%async_computation.5 | async-start | bytes 262144 | tf_op jit(solution)/shard_map/psum | solution.py:63
  853.6 132.3 %copy-start.3 = (bf16[16,4096]{1,0:T(8,128)(2,1)S(1)}, bf16[16,4096]{1,0:T(8,128)(2,1)}, u32[]{:S(2)}) copy-start(bf16[16,4096]{1,0:T(8,128)(2,1)} %all-reduce.16.cloned.1.call-done) | copy-start | bytes 393220
Sparse Core Ops, SparseCore 0:
  17.3 85.6 all-reduce.7
  112.0 58.4 all-reduce.9
  261.2 53.4 all-reduce.11
  485.0 53.4 all-reduce.13
  708.7 53.4 all-reduce.15
  932.4 53.4 all-reduce.17
where the time goes:
time: 1120 us
  blocking collectives  661 us (59%)
  waiting for transfers between devices  329 us (29%)
  matrix products  83.4 us (7%)
  between operations  26 us (2%)
  other arithmetic  18 us (2%)
    psum x4, blocking collectives, on_device(): lax.psum(row_products(features, direction_b).astype(jnp.bfloat16), 'feat')  290 us
    psum x7, blocking collectives, inner_total(): return lax.psum(value, 'feat')  273 us
    psum x4, waiting for transfers between devices, on_device(): lax.psum(column_products(curv_rows, features).astype(jnp.bfloat16), 'dp')  201 us
    psum x1, waiting for transfers between devices, on_device(): logits = lax.psum(row_products(features, weight_b), 'feat')  69.7 us
    psum x1, blocking collectives, on_device(): lax.psum(row_products(features, step_b).astype(jnp.bfloat16), 'feat')  69.6 us
    psum x1, waiting for transfers between devices, on_device(): lax.psum(grad_partial.astype(jnp.bfloat16), 'dp').astype(jnp.float32)  58.6 us
    dot_general x6, matrix products, row_products(): lax.dot_general(features, matrix_b, (((1,), (1,)), ((), ())), preferred_e...  48.4 us
    dot_general x5, matrix products, column_products(): lax.dot_general(rows_b, features, (((0,), (0,)), ((), ())), preferred_ele...  35 us
  transfers between devices with their start and end apart: 6, of which 6 were waited for; matrix products, arithmetic and copies ran while one was open for 0% of the time, Pallas kernels for 0%

commit v1 on v0

v1 whole, which is shorter than its diff:
```python
import functools

import jax
import jax.numpy as jnp
from jax import lax
from jax.experimental import pallas as pl
from jax.experimental.pallas import tpu as pltpu
from jax.sharding import PartitionSpec as P

CG_ITERS = 4
RIDGE_COEF = 0.1
NORM_GUARD = 1e-06

RING = 4
CORES = 2
SUBS = 2
LOAD = 6
MESH = pl.DeviceIdType.MESH
F32 = jnp.float32
BF16 = jnp.bfloat16


def dot(a, b, contract_a, contract_b):
    return lax.dot_general(
        a, b, (((contract_a,), (contract_b,)), ((), ())), preferred_element_type=F32
    )


def tile_sum(value):
    total = None
    for i in range(0, value.shape[0], 8):
        for j in range(0, value.shape[1], 128):
            part = value[i : i + 8, j : j + 128]
            total = part if total is None else total + part
    return total


def row_tile_sum(value):
    total = None
    for j in range(0, value.shape[1], 128):
        part = value[:, j : j + 128]
        total = part if total is None else total + part
    first = lax.broadcasted_iota(jnp.int32, (8, 128), 0) == 0
    return jnp.where(first, jnp.broadcast_to(total, (8, 128)), 0.0)


def whole_sum(tile):
    return jnp.sum(jnp.sum(tile, axis=0, keepdims=True), axis=1, keepdims=True)


def ordered_sum(ref, count):
    total = ref[0].astype(F32)
    for i in range(1, count):
        total = total + ref[i].astype(F32)
    return total


def kernel(
    x_hbm,
    w_hbm,
    labels_hbm,
    weights_hbm,
    step_ref,
    loss_ref,
    x_ref,
    xt_ref,
    wb_ref,
    labels_ref,
    weights_ref,
    r_ref,
    d_ref,
    prob_ref,
    rowscale_ref,
    curv_ref,
    sd_ref,
    acc_ref,
    part_ref,
    scal_ref,
    l1_ref,
    l2_ref,
    f1_ref,
    f2_ref,
    g1_ref,
    g2_ref,
    ca_ref,
    cb_ref,
    xs_ref,
    q_ref,
    wt_ref,
    load_sem,
    small_sem,
    l_send,
    l_recv,
    f_send,
    f_recv,
    g_send,
    g_recv,
    ca_send,
    ca_recv,
    cb_send,
    cb_recv,
    xs_send,
    xs_recv,
    q_send,
    q_recv,
    wt_send,
    wt_recv,
):
    dp = lax.axis_index("dp")
    ft = lax.axis_index("feat")
    px, core = dp // CORES, lax.rem(dp, CORES)
    pz, py = ft // RING, lax.rem(ft, RING)
    rows, cols = x_ref.shape
    half = rows // 2
    own_cols = cols // CORES
    sub = own_cols // SUBS
    load_rows = rows // LOAD

    def turn(at, by):
        return lax.rem(at + by, RING)

    def y_peer(k):
        return (dp, pz * RING + turn(py, k))

    def z_peer(k):
        return (dp, turn(pz, k) * RING + py)

    def x_peer(k):
        return (turn(px, k) * CORES + core, ft)

    def dp_peer(k):
        return (lax.rem(dp + k, RING * CORES), ft)

    partner = (px * CORES + (1 - core), ft)

    def load(i):
        start = pl.multiple_of(i * load_rows, load_rows)
        piece = pl.ds(start, load_rows)
        return pltpu.make_async_copy(x_hbm.at[piece], x_ref.at[piece], load_sem.at[i])

    small = [
        pltpu.make_async_copy(w_hbm, d_ref, small_sem.at[0]),
        pltpu.make_async_copy(labels_hbm, labels_ref, small_sem.at[1]),
        pltpu.make_async_copy(weights_hbm, weights_ref, small_sem.at[2]),
    ]
    for copy in small:
        copy.start()
    for i in range(LOAD):
        load(i).start()

    barrier = pltpu.get_barrier_semaphore()
    greeted = [dp_peer(k) for k in range(1, RING * CORES)]
    greeted += [y_peer(k) for k in range(1, RING)] + [z_peer(k) for k in range(1, RING)]
    for peer in greeted:
        pl.semaphore_signal(barrier, inc=1, device_id=peer, device_id_type=MESH)

    for copy in small:
        copy.wait()
    wb_ref[...] = d_ref[...].astype(BF16)
    r_ref[...] = jnp.zeros_like(r_ref)
    sd_ref[...] = jnp.zeros_like(sd_ref)
    step_ref[...] = jnp.zeros_like(step_ref)
    pl.semaphore_wait(barrier, len(greeted))

    def send(src, dst, send_sem, recv_sem, peer):
        copy = pltpu.make_async_remote_copy(
            src_ref=src,
            dst_ref=dst,
            send_sem=send_sem,
            recv_sem=recv_sem,
            device_id=peer,
            device_id_type=MESH,
        )
        copy.start()
        return copy

    def to_dp(ref, send_sem, recv_sem):
        return [
            send(ref.at[dp], ref.at[dp], send_sem.at[k - 1], recv_sem.at[k - 1], dp_peer(k))
            for k in range(1, RING * CORES)
        ]

    def to_ring(ref, at, send_sem, recv_sem, peer):
        return [
            send(ref.at[at], ref.at[at], send_sem.at[k - 1], recv_sem.at[k - 1], peer(k))
            for k in (2, 1, 3)
        ]

    at_1, peer_1 = (py, pz), (y_peer, z_peer)
    at_2, peer_2 = (pz, py), (z_peer, y_peer)

    wt_ref[dp] = row_tile_sum(weights_ref[...].astype(F32))
    wt_copies = to_dp(wt_ref, wt_send, wt_recv)

    def first_scores(i, _):
        load(i).wait()
        start = pl.multiple_of(i * load_rows, load_rows)
        acc_ref[:, pl.ds(start, load_rows)] = dot(
            wb_ref[...], x_ref[pl.ds(start, load_rows), :], 1, 1
        )
        return 0

    lax.fori_loop(0, LOAD, first_scores, 0)

    def turn_over(first, last):
        block = 512
        per_row = cols // block

        def one(i, _):
            row = pl.multiple_of((i // per_row) * block, block)
            col = pl.multiple_of(lax.rem(i, per_row) * block, block)
            xt_ref[pl.ds(col, block), pl.ds(row, block)] = x_ref[
                pl.ds(row, block), pl.ds(col, block)
            ].T
            return 0

        lax.fori_loop(first, last, one, 0)

    blocks = (rows // 512) * (cols // 512)

    copies_1 = []
    for h in range(2):
        l1_ref[h, at_1[h]] = acc_ref[:, h * half : (h + 1) * half]
        copies_1 += to_ring(l1_ref.at[h], at_1[h], l_send.at[0, h], l_recv.at[0, h], peer_1[h])
    turn_over(0, blocks // 2)
    copies_2 = []
    for h in range(2):
        for copy in copies_1[3 * h : 3 * h + 3]:
            copy.wait_recv()
        l2_ref[h, at_2[h]] = ordered_sum(l1_ref.at[h], RING)
        copies_2 += to_ring(l2_ref.at[h], at_2[h], l_send.at[1, h], l_recv.at[1, h], peer_2[h])
    turn_over(blocks // 2, blocks)
    for copy in wt_copies:
        copy.wait()
    weight_total = whole_sum(ordered_sum(wt_ref, RING * CORES))

    loss_tile = None
    classes = lax.broadcasted_iota(jnp.int32, (w_hbm.shape[0], half), 0)
    for h in range(2):
        for copy in copies_2[3 * h : 3 * h + 3]:
            copy.wait_recv()
        at = slice(h * half, (h + 1) * half)
        logits = ordered_sum(l2_ref.at[h], RING)
        row_top = jnp.max(logits, axis=0, keepdims=True)
        shifted = jnp.exp(logits - row_top)
        summed = jnp.sum(shifted, axis=0, keepdims=True)
        class_prob = shifted / summed
        log_total = row_top + jnp.log(summed)
        row_weight = weights_ref[:, at].astype(F32)
        onehot = (labels_ref[:, at] == classes).astype(F32)
        picked = jnp.sum(logits * onehot, axis=0, keepdims=True)
        part = row_tile_sum(row_weight * (log_total - picked))
        loss_tile = part if loss_tile is None else loss_tile + part
        row_scale = row_weight / weight_total
        prob_ref[:, at] = class_prob
        rowscale_ref[:, at] = row_scale
        curv_ref[:, at] = (row_scale * (class_prob - onehot)).astype(BF16)
    for copy in copies_1 + copies_2:
        copy.wait_send()

    q_ref[0, dp] = loss_tile
    to_dp(q_ref.at[0], q_send.at[0], q_recv.at[0])

    def wait_dp(slot):
        for k in range(1, RING * CORES):
            pltpu.make_async_remote_copy(
                src_ref=q_ref.at[slot, dp],
                dst_ref=q_ref.at[slot, dp],
                send_sem=q_send.at[slot, k - 1],
                recv_sem=q_recv.at[slot, k - 1],
                device_id=dp_peer(k),
                device_id_type=MESH,
            ).wait()
        return whole_sum(ordered_sum(q_ref.at[slot], RING * CORES))

    one = jnp.ones((8, 128), F32)
    scal_ref[0] = one
    scal_ref[1] = one
    scal_ref[2] = one
    mine = core * own_cols
    theirs = (1 - core) * own_cols

    def iteration(it, _):
        slot = lax.rem(it, 2)

        ca_copies = []
        for s in range(SUBS):
            start = pl.multiple_of(theirs + s * sub, sub)
            ca_ref[slot, 0, s] = dot(curv_ref[...], x_ref[:, pl.ds(start, sub)], 1, 0).astype(BF16)
            ca_copies.append(
                send(
                    ca_ref.at[slot, 0, s],
                    ca_ref.at[slot, 1, s],
                    ca_send.at[slot, s],
                    ca_recv.at[slot, s],
                    partner,
                )
            )
        xs_copies = []
        for s in range(SUBS):
            start = pl.multiple_of(mine + s * sub, sub)
            part = dot(curv_ref[...], x_ref[:, pl.ds(start, sub)], 1, 0)
            ca_copies[s].wait_recv()
            xs_ref[slot, s, px] = (part + ca_ref[slot, 1, s].astype(F32)).astype(BF16)
            xs_copies.append(
                to_ring(
                    xs_ref.at[slot, s], px, xs_send.at[slot, s], xs_recv.at[slot, s], x_peer
                )
            )

        reduced = wait_dp(slot)
        beta = scal_ref[0, 0:1, 0:1]
        res_norm = scal_ref[1, 0:1, 0:1]
        dir_norm = scal_ref[2, 0:1, 0:1]
        first = it == 0

        @pl.when(first)
        def _():
            loss_ref[...] = reduced / weight_total

        step_size = jnp.where(first, 1.0, res_norm / (reduced + RIDGE_COEF * dir_norm))
        step_ref[...] = step_ref[...] + step_size * sd_ref[...]

        def advance(start, image, tiles):
            at = pl.ds(pl.multiple_of(start, sub), sub)
            residual = r_ref[:, at]
            direction = residual + beta * d_ref[:, at]
            residual = residual - step_size * (image.astype(F32) + RIDGE_COEF * direction)
            r_ref[:, at] = residual
            d_ref[:, at] = direction
            scores = dot(residual.astype(BF16), xt_ref[at, :], 1, 0)
            both = (tile_sum(residual * residual), tile_sum(residual * direction))
            return scores, both if tiles is None else tuple(a + b for a, b in zip(tiles, both))

        cb_copies = []
        tiles = None
        for s in range(SUBS):
            for copy in xs_copies[s]:
                copy.wait_recv()
            cb_ref[slot, 0, s] = ordered_sum(xs_ref.at[slot, s], RING).astype(BF16)
            cb_copies.append(
                send(
                    cb_ref.at[slot, 0, s],
                    cb_ref.at[slot, 1, s],
                    cb_send.at[slot, s],
                    cb_recv.at[slot, s],
                    partner,
                )
            )
            scores, tiles = advance(mine + s * sub, cb_ref[slot, 0, s], tiles)
            acc_ref[...] = scores if s == 0 else acc_ref[...] + scores
        for s in range(SUBS):
            cb_copies[s].wait_recv()
            scores, tiles = advance(theirs + s * sub, cb_ref[slot, 1, s], tiles)
            acc_ref[...] = acc_ref[...] + scores

        copies_1, copies_2 = [], []
        g1_ref[slot, py, 0] = tiles[0]
        g1_ref[slot, py, 1] = tiles[1]
        for h in range(2):
            f1_ref[slot, h, at_1[h]] = acc_ref[:, h * half : (h + 1) * half].astype(BF16)
            copies_1 += to_ring(
                f1_ref.at[slot, h], at_1[h], f_send.at[slot, 0, h], f_recv.at[slot, 0, h], peer_1[h]
            )
        small_1 = to_ring(g1_ref.at[slot], py, g_send.at[slot, 0], g_recv.at[slot, 0], y_peer)
        for h in range(2):
            for copy in copies_1[3 * h : 3 * h + 3]:
                copy.wait_recv()
            f2_ref[slot, h, at_2[h]] = ordered_sum(f1_ref.at[slot, h], RING).astype(BF16)
            copies_2 += to_ring(
                f2_ref.at[slot, h], at_2[h], f_send.at[slot, 1, h], f_recv.at[slot, 1, h], peer_2[h]
            )
        for copy in small_1:
            copy.wait_recv()
        g2_ref[slot, pz] = ordered_sum(g1_ref.at[slot], RING)
        small_2 = to_ring(g2_ref.at[slot], pz, g_send.at[slot, 1], g_recv.at[slot, 1], z_peer)
        for copies in xs_copies:
            for copy in copies:
                copy.wait_send()
        for copy in ca_copies + cb_copies + copies_1 + small_1:
            copy.wait_send()

        for copy in small_2:
            copy.wait()
        sums = ordered_sum(g2_ref.at[slot], RING)
        new_norm = whole_sum(sums[0])
        cross = whole_sum(sums[1])
        new_beta = jnp.where(first, 0.0, new_norm / (res_norm + NORM_GUARD))
        new_dir_norm = new_norm + new_beta * (2.0 * cross + new_beta * dir_norm)
        scal_ref[0] = jnp.broadcast_to(new_beta, (8, 128))
        scal_ref[1] = jnp.broadcast_to(new_norm, (8, 128))
        scal_ref[2] = jnp.broadcast_to(new_dir_norm, (8, 128))
        curvature = None
        for h in range(2):
            for copy in copies_2[3 * h : 3 * h + 3]:
                copy.wait()
            at = slice(h * half, (h + 1) * half)
            scores = ordered_sum(f2_ref.at[slot, h], RING) + new_beta * sd_ref[:, at]
            sd_ref[:, at] = scores
            class_prob = prob_ref[:, at]
            mixed = jnp.sum(class_prob * scores, axis=0, keepdims=True)
            curv = (rowscale_ref[:, at] * class_prob * (scores - mixed)).astype(BF16)
            curv_ref[:, at] = curv
            part = tile_sum(scores * curv.astype(F32))
            curvature = part if curvature is None else curvature + part
        q_ref[1 - slot, dp] = curvature
        to_dp(q_ref.at[1 - slot], q_send.at[1 - slot], q_recv.at[1 - slot])
        return 0

    lax.fori_loop(0, CG_ITERS, iteration, 0)

    last = CG_ITERS % 2
    reduced = wait_dp(last)
    step_size = scal_ref[1, 0:1, 0:1] / (reduced + RIDGE_COEF * scal_ref[2, 0:1, 0:1])
    step_ref[...] = step_ref[...] + step_size * sd_ref[...]


def on_device(features, weight, labels, sample_weight):
    rows, cols = features.shape
    classes = weight.shape[0]
    half, sub = rows // 2, cols // CORES // SUBS
    any_space = pl.BlockSpec(memory_space=pl.ANY)
    vmem = pl.BlockSpec(memory_space=pltpu.VMEM)
    dma = pltpu.SemaphoreType.DMA
    peers = RING * CORES - 1
    step, loss = pl.pallas_call(
        kernel,
        out_shape=(
            jax.ShapeDtypeStruct((classes, rows), F32),
            jax.ShapeDtypeStruct((1, 1), F32),
        ),
        in_specs=[any_space] * 4,
        out_specs=(vmem, vmem),
        scratch_shapes=[
            pltpu.VMEM((rows, cols), BF16),
            pltpu.VMEM((cols, rows), BF16),
            pltpu.VMEM((classes, cols), BF16),
            pltpu.VMEM((1, rows), jnp.int32),
            pltpu.VMEM((1, rows), jnp.int32),
            pltpu.VMEM((classes, cols), F32),
            pltpu.VMEM((classes, cols), F32),
            pltpu.VMEM((classes, rows), F32),
            pltpu.VMEM((1, rows), F32),
            pltpu.VMEM((classes, rows), BF16),
            pltpu.VMEM((classes, rows), F32),
            pltpu.VMEM((classes, rows), F32),
            pltpu.VMEM((classes, sub), F32),
            pltpu.VMEM((3, 8, 128), F32),
            pltpu.VMEM((2, RING, classes, half), F32),
            pltpu.VMEM((2, RING, classes, half), F32),
            pltpu.VMEM((2, 2, RING, classes, half), BF16),
            pltpu.VMEM((2, 2, RING, classes, half), BF16),
            pltpu.VMEM((2, RING, 2, 8, 128), F32),
            pltpu.VMEM((2, RING, 2, 8, 128), F32),
            pltpu.VMEM((2, 2, SUBS, classes, sub), BF16),
            pltpu.VMEM((2, 2, SUBS, classes, sub), BF16),
            pltpu.VMEM((2, SUBS, RING, classes, sub), BF16),
            pltpu.VMEM((2, RING * CORES, 8, 128), F32),
            pltpu.VMEM((RING * CORES, 8, 128), F32),
            dma((LOAD,)),
            dma((3,)),
            dma((2, 2, 3)),
            dma((2, 2, 3)),
            dma((2, 2, 2, 3)),
            dma((2, 2, 2, 3)),
            dma((2, 2, 3)),
            dma((2, 2, 3)),
            dma((2, SUBS)),
            dma((2, SUBS)),
            dma((2, SUBS)),
            dma((2, SUBS)),
            dma((2, SUBS, 3)),
            dma((2, SUBS, 3)),
            dma((2, peers)),
            dma((2, peers)),
            dma((peers,)),
            dma((peers,)),
        ],
        compiler_params=pltpu.CompilerParams(
            collective_id=0, has_side_effects=True, vmem_limit_bytes=56 * 1024 * 1024
        ),
        name="newton_cg",
    )(features, weight, labels.reshape(1, rows), sample_weight.reshape(1, rows))
    return step.T, loss.reshape(())


def solution(mesh):
    in_specs = (P("dp", "feat"), P(None, "feat"), P("dp"), P("dp"))
    out_specs = (P("dp", None), P())
    return jax.shard_map(
        on_device, mesh=mesh, in_specs=in_specs, out_specs=out_specs, check_vma=False
    )
```

time: 1120 us -> 103 us (0.09)
  blocking collectives: 661 us -> 0 us
  waiting for transfers between devices: 329 us -> 0 us
  Pallas kernels: 0 us -> 95.5 us
  matrix products: 83.4 us -> 0 us
  between operations: 26 us -> 2.33 us
  other arithmetic: 18 us -> 0 us
    psum x14 -> x0, blocking collectives: 661 us -> none  [the longest x4 290 us: on_device(): lax.psum(row_products(features, direction_b).astype(jnp.bfloat16), 'feat')]
    psum x6 -> x0, waiting for transfers between devices: 329 us -> none  [the longest x4 201 us: on_device(): lax.psum(column_products(curv_rows, features).astype(jnp.bfloat16), 'dp')]
    pallas_call x0 -> x1, Pallas kernels: none -> 95.5 us  [on_device(): pl.pallas_call(kernel, out_shape=(jax.ShapeDtypeStruct((classes, rows), F...]
    dot_general x11 -> x0, matrix products: 83.4 us -> none  [the longest x6 48.4 us: row_products(): lax.dot_general(features, matrix_b, (((1,), (1,)), ((), ())), preferred_e...]
    reduce_sum x14 -> x0, other arithmetic: 14.9 us -> none  [the longest x4 6.78 us: on_device(): step_size = res_norm / inner_total(jnp.sum(direction * hess_image))]
  transfers between devices with their start and end apart: 6 -> 0, of which waited for: 6 -> 0; matrix products, arithmetic and copies ran while one was open for 0% -> 0% of each run, Pallas kernels for 0% -> 0%
where the time goes in v1:
time: 103 us; the launch traced here: 102 us
  Pallas kernels  95.5 us (93%)
  local copies, waits for them, and re-layouts  4.14 us (4%)
  between operations  2.33 us (2%)
    pallas_call x1, Pallas kernels, on_device(): pl.pallas_call(kernel, out_shape=(jax.ShapeDtypeStruct((classes, rows), F...  95.5 us

profile of v1, /device:TPU:0, one launch (start us, length us, event | category | flops | bytes accessed | tf_op | source)
XLA Modules:
  0.0 102.0 jit_solution(6463335078881851810)
XLA Ops:
  0.6 1.3 %reshape.13.labels_hbm = s32[1,1536]{1,0:T(1,128)} reshape(s32[1536]{0:T(1024)} %param.6) | data formatting | bytes 12288 | tf_op jit(solution)/shard_map/reshape | solution.py:483
  1.9 1.3 %reshape.14.weights_hbm = s32[1,1536]{1,0:T(1,128)} reshape(s32[1536]{0:T(1024)} %param.7) | data formatting | bytes 12288 | tf_op jit(solution)/shard_map/reshape | solution.py:483
  3.2 95.5 %newton_cg.1 = (f32[16,1536]{1,0:T(8,128)}, f32[1,1]{1,0:T(1,128)}) custom-call(bf16[1536,4096]{1,0:T(8,128)(2,1)} %x_hbm.1, f32[16,4096]{1,0:T(8,128)} %w_hbm.1, s32[1,1536]{1,0:T(1,128)} %reshape.13.labels_hbm, s32[1,1536]{1,0:T(1,128)} %reshape.14.weights_hbm), custom_call_target="tpu_custom_call" | custom-call | tf_op jit(solution)/shard_map/newton_cg/pallas_call | solution.py:426
  98.7 1.5 %copy.8 = f32[1536,16]{0,1:T(8,128)} copy(f32[1536,16]{0,1:T(8,128)} %bitcast.2) | data formatting | bytes 196608

commit v2 on v1

v2 whole, which is shorter than its diff:
```python
import functools

import jax
import jax.numpy as jnp
from jax import lax
from jax.experimental import pallas as pl
from jax.experimental.pallas import tpu as pltpu
from jax.sharding import PartitionSpec as P

CG_ITERS = 4
RIDGE_COEF = 0.1
NORM_GUARD = 1e-06

RING = 4
CORES = 2
SUBS = (512, 1024, 512)
LOAD = (256, 512, 256, 512)
EARLY = 2
MESH = pl.DeviceIdType.MESH
F32 = jnp.float32
BF16 = jnp.bfloat16


def dot(a, b, contract_a, contract_b):
    return lax.dot_general(
        a, b, (((contract_a,), (contract_b,)), ((), ())), preferred_element_type=F32
    )


def tile_sum(value):
    total = None
    for i in range(0, value.shape[0], 8):
        for j in range(0, value.shape[1], 128):
            part = value[i : i + 8, j : j + 128]
            total = part if total is None else total + part
    return total


def row_tile_sum(value):
    total = None
    for j in range(0, value.shape[1], 128):
        part = value[:, j : j + 128]
        total = part if total is None else total + part
    first = lax.broadcasted_iota(jnp.int32, (8, 128), 0) == 0
    return jnp.where(first, jnp.broadcast_to(total, (8, 128)), 0.0)


def whole_sum(tile):
    return jnp.sum(jnp.sum(tile, axis=0, keepdims=True), axis=1, keepdims=True)


def row_of(ref, start, size):
    return ref[start : start + size].reshape(1, size)


def ordered_sum(ref, count):
    total = ref[0].astype(F32)
    for i in range(1, count):
        total = total + ref[i].astype(F32)
    return total


def kernel(
    x_hbm,
    w_hbm,
    labels_hbm,
    weights_hbm,
    step_ref,
    loss_hbm,
    x_ref,
    xt_ref,
    wb_ref,
    labels_ref,
    weights_ref,
    loss_ref,
    r_ref,
    d_ref,
    prob_ref,
    rowscale_ref,
    curv_ref,
    sd_ref,
    acc_ref,
    scal_ref,
    l1_ref,
    l2_ref,
    f1_ref,
    f2_ref,
    g1_ref,
    g2_ref,
    ca_ref,
    cb_ref,
    xs_ref,
    q_ref,
    wt_ref,
    load_sem,
    small_sem,
    l_send,
    l_recv,
    f_send,
    f_recv,
    g_send,
    g_recv,
    ca_send,
    ca_recv,
    cb_send,
    cb_recv,
    xs_send,
    xs_recv,
    q_send,
    q_recv,
    wt_send,
    wt_recv,
):
    dp = lax.axis_index("dp")
    ft = lax.axis_index("feat")
    px, core = dp // CORES, lax.rem(dp, CORES)
    pz, py = ft // RING, lax.rem(ft, RING)
    rows, cols = x_ref.shape
    half = rows // 2
    own_cols = cols // CORES
    pieces = [(sum(SUBS[:s]), SUBS[s]) for s in range(len(SUBS))]

    def turn(at, by):
        return lax.rem(at + by, RING)

    def y_peer(k):
        return (dp, pz * RING + turn(py, k))

    def z_peer(k):
        return (dp, turn(pz, k) * RING + py)

    def x_peer(k):
        return (turn(px, k) * CORES + core, ft)

    def dp_peer(k):
        return (lax.rem(dp + k, RING * CORES), ft)

    partner = (px * CORES + (1 - core), ft)

    def load(i):
        piece = pl.ds(sum(LOAD[:i]), LOAD[i])
        return pltpu.make_async_copy(x_hbm.at[piece], x_ref.at[piece], load_sem.at[i])

    small = [
        pltpu.make_async_copy(w_hbm, d_ref, small_sem.at[0]),
        pltpu.make_async_copy(labels_hbm, labels_ref, small_sem.at[1]),
        pltpu.make_async_copy(weights_hbm, weights_ref, small_sem.at[2]),
    ]
    store_loss = pltpu.make_async_copy(loss_ref, loss_hbm, small_sem.at[3])
    small[0].start()
    for i in range(EARLY):
        load(i).start()
    small[1].start()
    small[2].start()

    barrier = pltpu.get_barrier_semaphore()
    greeted = [dp_peer(k) for k in range(1, RING * CORES)]
    greeted += [y_peer(k) for k in range(1, RING)] + [z_peer(k) for k in range(1, RING)]
    for peer in greeted:
        pl.semaphore_signal(barrier, inc=1, device_id=peer, device_id_type=MESH)

    small[0].wait()
    for i in range(EARLY, len(LOAD)):
        load(i).start()
    wb_ref[...] = d_ref[...].astype(BF16)
    r_ref[...] = jnp.zeros_like(r_ref)
    sd_ref[...] = jnp.zeros_like(sd_ref)
    step_ref[...] = jnp.zeros_like(step_ref)
    def send(src, dst, send_sem, recv_sem, peer):
        copy = pltpu.make_async_remote_copy(
            src_ref=src,
            dst_ref=dst,
            send_sem=send_sem,
            recv_sem=recv_sem,
            device_id=peer,
            device_id_type=MESH,
        )
        copy.start()
        return copy

    def to_dp(ref, send_sem, recv_sem):
        for k in range(1, RING * CORES):
            send(ref.at[dp], ref.at[dp], send_sem, recv_sem, dp_peer(k))

    def to_ring(ref, at, send_sem, recv_sem, peer):
        for k in (2, 1, 3):
            send(ref.at[at], ref.at[at], send_sem, recv_sem, peer(k))

    def wait_group(ref, sem):
        others = ref.at[pl.ds(0, ref.shape[0] - 1)]
        pltpu.make_async_copy(others, others, sem).wait()

    at_1, peer_1 = (py, pz), (y_peer, z_peer)
    at_2, peer_2 = (pz, py), (z_peer, y_peer)

    for i in range(len(LOAD)):
        start = sum(LOAD[:i])
        load(i).wait()
        h, into = divmod(start, half)
        l1_ref[h, at_1[h], :, into : into + LOAD[i]] = dot(
            wb_ref[...], x_ref[start : start + LOAD[i], :], 1, 1
        )
        if into + LOAD[i] == half:
            if h == 0:
                pl.semaphore_wait(barrier, len(greeted))
            to_ring(l1_ref.at[h], at_1[h], l_send.at[0, h], l_recv.at[0, h], peer_1[h])
    small[1].wait()
    small[2].wait()
    wt_ref[dp] = row_tile_sum(row_of(weights_ref, 0, rows).astype(F32))
    to_dp(wt_ref, wt_send.at[0], wt_recv.at[0])

    def turn_over(first, last):
        block = 512
        per_row = cols // block

        def one(i, _):
            row = pl.multiple_of((i // per_row) * block, block)
            col = pl.multiple_of(lax.rem(i, per_row) * block, block)
            xt_ref[pl.ds(col, block), pl.ds(row, block)] = x_ref[
                pl.ds(row, block), pl.ds(col, block)
            ].T
            return 0

        lax.fori_loop(first, last, one, 0)

    blocks = (rows // 512) * (cols // 512)

    turn_over(0, blocks // 2)
    for h in range(2):
        wait_group(l1_ref.at[h], l_recv.at[0, h])
        l2_ref[h, at_2[h]] = ordered_sum(l1_ref.at[h], RING)
        to_ring(l2_ref.at[h], at_2[h], l_send.at[1, h], l_recv.at[1, h], peer_2[h])
    turn_over(blocks // 2, blocks)
    wait_group(wt_ref, wt_recv.at[0])
    weight_total = whole_sum(ordered_sum(wt_ref, RING * CORES))

    loss_tile = None
    classes = lax.broadcasted_iota(jnp.int32, (w_hbm.shape[0], half), 0)
    for h in range(2):
        wait_group(l2_ref.at[h], l_recv.at[1, h])
        at = slice(h * half, (h + 1) * half)
        logits = ordered_sum(l2_ref.at[h], RING)
        row_top = jnp.max(logits, axis=0, keepdims=True)
        shifted = jnp.exp(logits - row_top)
        summed = jnp.sum(shifted, axis=0, keepdims=True)
        class_prob = shifted / summed
        log_total = row_top + jnp.log(summed)
        row_weight = row_of(weights_ref, h * half, half).astype(F32)
        onehot = (row_of(labels_ref, h * half, half) == classes).astype(F32)
        picked = jnp.sum(logits * onehot, axis=0, keepdims=True)
        part = row_tile_sum(row_weight * (log_total - picked))
        loss_tile = part if loss_tile is None else loss_tile + part
        row_scale = row_weight / weight_total
        prob_ref[:, at] = class_prob
        rowscale_ref[:, at] = row_scale
        curv_ref[:, at] = (row_scale * (class_prob - onehot)).astype(BF16)
    q_ref[0, dp] = loss_tile
    to_dp(q_ref.at[0], q_send.at[0], q_recv.at[0])
    for h in range(2):
        wait_group(l1_ref.at[h], l_send.at[0, h])
        wait_group(l2_ref.at[h], l_send.at[1, h])
    wait_group(wt_ref, wt_send.at[0])

    def wait_dp(slot):
        wait_group(q_ref.at[slot], q_recv.at[slot])
        wait_group(q_ref.at[slot], q_send.at[slot])
        return whole_sum(ordered_sum(q_ref.at[slot], RING * CORES))

    one = jnp.ones((8, 128), F32)
    scal_ref[0] = one
    scal_ref[1] = one
    scal_ref[2] = one
    mine = core * own_cols
    theirs = (1 - core) * own_cols

    def iteration(it, _):
        slot = lax.rem(it, 2)

        ca_copies = []
        for s, (at, size) in enumerate(pieces):
            start = pl.multiple_of(theirs + at, 128)
            piece = pl.ds(at, size)
            ca_ref[slot, 0, :, piece] = dot(curv_ref[...], x_ref[:, pl.ds(start, size)], 1, 0).astype(
                BF16
            )
            ca_copies.append(
                send(
                    ca_ref.at[slot, 0, :, piece],
                    ca_ref.at[slot, 1, :, piece],
                    ca_send.at[slot, s],
                    ca_recv.at[slot, s],
                    partner,
                )
            )
        for s, (at, size) in enumerate(pieces):
            start = pl.multiple_of(mine + at, 128)
            piece = pl.ds(at, size)
            part = dot(curv_ref[...], x_ref[:, pl.ds(start, size)], 1, 0)
            ca_copies[s].wait_recv()
            xs_ref[slot, px, :, piece] = (part + ca_ref[slot, 1, :, piece].astype(F32)).astype(BF16)
            to_ring(
                xs_ref.at[slot, :, :, piece], px, xs_send.at[slot, s], xs_recv.at[slot, s], x_peer
            )

        reduced = wait_dp(slot)
        beta = scal_ref[0, 0:1, 0:1]
        res_norm = scal_ref[1, 0:1, 0:1]
        dir_norm = scal_ref[2, 0:1, 0:1]
        first = it == 0

        @pl.when(first)
        def _():
            loss_ref[...] = reduced / weight_total
            store_loss.start()

        step_size = jnp.where(first, 1.0, res_norm / (reduced + RIDGE_COEF * dir_norm))
        step_ref[...] = step_ref[...] + step_size * sd_ref[...]

        def advance(start, size, image):
            at = pl.ds(pl.multiple_of(start, 128), size)
            residual = r_ref[:, at]
            direction = residual + beta * d_ref[:, at]
            residual = residual - step_size * (image.astype(F32) + RIDGE_COEF * direction)
            r_ref[:, at] = residual
            d_ref[:, at] = direction
            tiles.append((tile_sum(residual * residual), tile_sum(residual * direction)))
            return residual.astype(BF16), xt_ref.at[at]

        tiles = []
        cb_copies = []
        for s, (at, size) in enumerate(pieces):
            piece = pl.ds(at, size)
            wait_group(xs_ref.at[slot, :, :, piece], xs_recv.at[slot, s])
            image = ordered_sum(xs_ref.at[slot, :, :, piece], RING).astype(BF16)
            cb_ref[slot, 0, :, piece] = image
            cb_copies.append(
                send(
                    cb_ref.at[slot, 0, :, piece],
                    cb_ref.at[slot, 1, :, piece],
                    cb_send.at[slot, s],
                    cb_recv.at[slot, s],
                    partner,
                )
            )
            residual, turned = advance(mine + at, size, image)
            scores = dot(residual, turned[...], 1, 0)
            acc_ref[...] = scores if s == 0 else acc_ref[...] + scores
        for s, (at, size) in enumerate(pieces):
            cb_copies[s].wait_recv()
            residual, turned = advance(theirs + at, size, cb_ref[slot, 1, :, pl.ds(at, size)])
            if s < len(pieces) - 1:
                acc_ref[...] = acc_ref[...] + dot(residual, turned[...], 1, 0)

        for i in range(2):
            total = tiles[0][i]
            for both in tiles[1:]:
                total = total + both[i]
            g1_ref[slot, py, i] = total
        to_ring(g1_ref.at[slot], py, g_send.at[slot, 0], g_recv.at[slot, 0], y_peer)
        for h in range(2):
            at = slice(h * half, (h + 1) * half)
            f1_ref[slot, h, at_1[h]] = (acc_ref[:, at] + dot(residual, turned[:, at], 1, 0)).astype(
                BF16
            )
            to_ring(
                f1_ref.at[slot, h], at_1[h], f_send.at[slot, 0, h], f_recv.at[slot, 0, h], peer_1[h]
            )
        wait_group(g1_ref.at[slot], g_recv.at[slot, 0])
        g2_ref[slot, pz] = ordered_sum(g1_ref.at[slot], RING)
        to_ring(g2_ref.at[slot], pz, g_send.at[slot, 1], g_recv.at[slot, 1], z_peer)
        for h in range(2):
            wait_group(f1_ref.at[slot, h], f_recv.at[slot, 0, h])
            f2_ref[slot, h, at_2[h]] = ordered_sum(f1_ref.at[slot, h], RING).astype(BF16)
            to_ring(
                f2_ref.at[slot, h], at_2[h], f_send.at[slot, 1, h], f_recv.at[slot, 1, h], peer_2[h]
            )
        for s, (at, size) in enumerate(pieces):
            wait_group(xs_ref.at[slot, :, :, pl.ds(at, size)], xs_send.at[slot, s])
        for copy in ca_copies + cb_copies:
            copy.wait_send()
        for h in range(2):
            wait_group(f1_ref.at[slot, h], f_send.at[slot, 0, h])
        wait_group(g1_ref.at[slot], g_send.at[slot, 0])

        wait_group(g2_ref.at[slot], g_recv.at[slot, 1])
        wait_group(g2_ref.at[slot], g_send.at[slot, 1])
        sums = ordered_sum(g2_ref.at[slot], RING)
        new_norm = whole_sum(sums[0])
        cross = whole_sum(sums[1])
        new_beta = jnp.where(first, 0.0, new_norm / (res_norm + NORM_GUARD))
        new_dir_norm = new_norm + new_beta * (2.0 * cross + new_beta * dir_norm)
        scal_ref[0] = jnp.broadcast_to(new_beta, (8, 128))
        scal_ref[1] = jnp.broadcast_to(new_norm, (8, 128))
        scal_ref[2] = jnp.broadcast_to(new_dir_norm, (8, 128))
        curvature = None
        for h in range(2):
            wait_group(f2_ref.at[slot, h], f_recv.at[slot, 1, h])
            at = slice(h * half, (h + 1) * half)
            scores = ordered_sum(f2_ref.at[slot, h], RING) + new_beta * sd_ref[:, at]
            sd_ref[:, at] = scores
            class_prob = prob_ref[:, at]
            mixed = jnp.sum(class_prob * scores, axis=0, keepdims=True)
            curv = (rowscale_ref[:, at] * class_prob * (scores - mixed)).astype(BF16)
            curv_ref[:, at] = curv
            part = tile_sum(scores * curv.astype(F32))
            curvature = part if curvature is None else curvature + part
        q_ref[1 - slot, dp] = curvature
        to_dp(q_ref.at[1 - slot], q_send.at[1 - slot], q_recv.at[1 - slot])
        for h in range(2):
            wait_group(f2_ref.at[slot, h], f_send.at[slot, 1, h])
        return 0

    lax.fori_loop(0, CG_ITERS, iteration, 0)

    store_loss.wait()
    last = CG_ITERS % 2
    reduced = wait_dp(last)
    step_size = scal_ref[1, 0:1, 0:1] / (reduced + RIDGE_COEF * scal_ref[2, 0:1, 0:1])
    step_ref[...] = step_ref[...] + step_size * sd_ref[...]


def on_device(features, weight, labels, sample_weight):
    arrays = (features, weight, labels, sample_weight)
    rows, cols = features.shape
    classes = weight.shape[0]
    half, own_cols = rows // 2, cols // CORES
    hbm = pl.BlockSpec(memory_space=pltpu.HBM)
    vmem = pl.BlockSpec(memory_space=pltpu.VMEM)
    dma = pltpu.SemaphoreType.DMA
    subs = len(SUBS)
    step, loss = pl.pallas_call(
        kernel,
        out_shape=(
            jax.ShapeDtypeStruct((classes, rows), F32),
            jax.ShapeDtypeStruct((1, 1), F32),
        ),
        in_specs=[hbm] * 4,
        out_specs=(vmem, hbm),
        scratch_shapes=[
            pltpu.VMEM((rows, cols), BF16),
            pltpu.VMEM((cols, rows), BF16),
            pltpu.VMEM((classes, cols), BF16),
            pltpu.VMEM((rows,), jnp.int32),
            pltpu.VMEM((rows,), jnp.int32),
            pltpu.VMEM((1, 1), F32),
            pltpu.VMEM((classes, cols), F32),
            pltpu.VMEM((classes, cols), F32),
            pltpu.VMEM((classes, rows), F32),
            pltpu.VMEM((1, rows), F32),
            pltpu.VMEM((classes, rows), BF16),
            pltpu.VMEM((classes, rows), F32),
            pltpu.VMEM((classes, rows), F32),
            pltpu.VMEM((3, 8, 128), F32),
            pltpu.VMEM((2, RING, classes, half), F32),
            pltpu.VMEM((2, RING, classes, half), F32),
            pltpu.VMEM((2, 2, RING, classes, half), BF16),
            pltpu.VMEM((2, 2, RING, classes, half), BF16),
            pltpu.VMEM((2, RING, 2, 8, 128), F32),
            pltpu.VMEM((2, RING, 2, 8, 128), F32),
            pltpu.VMEM((2, 2, classes, own_cols), BF16),
            pltpu.VMEM((2, 2, classes, own_cols), BF16),
            pltpu.VMEM((2, RING, classes, own_cols), BF16),
            pltpu.VMEM((2, RING * CORES, 8, 128), F32),
            pltpu.VMEM((RING * CORES, 8, 128), F32),
            dma((len(LOAD),)),
            dma((4,)),
            dma((2, 2)),
            dma((2, 2)),
            dma((2, 2, 2)),
            dma((2, 2, 2)),
            dma((2, 2)),
            dma((2, 2)),
            dma((2, subs)),
            dma((2, subs)),
            dma((2, subs)),
            dma((2, subs)),
            dma((2, subs)),
            dma((2, subs)),
            dma((2,)),
            dma((2,)),
            dma((1,)),
            dma((1,)),
        ],
        compiler_params=pltpu.CompilerParams(
            collective_id=0, has_side_effects=True, vmem_limit_bytes=44 * 1024 * 1024
        ),
        name="newton_cg",
    )(*(pltpu.with_memory_space_constraint(a, pltpu.HBM) for a in arrays))
    return step.T, loss.reshape(())


def solution(mesh):
    in_specs = (P("dp", "feat"), P(None, "feat"), P("dp"), P("dp"))
    out_specs = (P("dp", None), P())
    return jax.shard_map(
        on_device, mesh=mesh, in_specs=in_specs, out_specs=out_specs, check_vma=False
    )
```

time: 103 us -> 93.6 us (0.909)
  Pallas kernels: 95.5 us -> 89.5 us
  local copies, waits for them, and re-layouts: 4.14 us -> 0.64 us
    pallas_call x1, Pallas kernels: 95.5 us -> 89.5 us  [on_device(): pl.pallas_call(kernel, out_shape=(jax.ShapeDtypeStruct((classes, rows), F...]
    reshape x2 -> x0, local copies, waits for them, and re-layouts: 2.6 us -> none  [the longest x1 1.3 us: on_device(): sample_weight.reshape(1, rows)]
where the time goes in v2:
time: 93.6 us; the launch traced here: 92.5 us
  Pallas kernels  89.5 us (96%)
  between operations  2.33 us (2%)
    pallas_call x1, Pallas kernels, on_device(): pl.pallas_call(kernel, out_shape=(jax.ShapeDtypeStruct((classes, rows), F...  89.5 us

profile of v2, /device:TPU:0, one launch (start us, length us, event | category | flops | bytes accessed | tf_op | source)
XLA Modules:
  0.0 92.5 jit_solution(1862867263354884511)
XLA Ops:
  0.6 89.5 %newton_cg.1 = (f32[16,1536]{1,0:T(8,128)S(1)}, f32[1,1]{1,0:T(1,128)}) custom-call(bf16[1536,4096]{1,0:T(8,128)(2,1)} %x_hbm.1, f32[16,4096]{1,0:T(8,128)} %w_hbm.1, s32[1536]{0:T(1024)} %labels_hbm.1, s32[1536]{0:T(1024)} %weights_hbm.1), custom_call_target="tpu_custom_call" | custom-call | tf_op jit(solution)/shard_map/newton_cg/pallas_call | solution.py:431
  90.1 0.6 copy.8

commit v3 on v2

--- a/solution.py
+++ b/solution.py
@@ -14,7 +14,8 @@
 RING = 4
 CORES = 2
 SUBS = (512, 1024, 512)
-LOAD = (256, 512, 256, 512)
+BLOCK = 512
+WIDE = 2
 EARLY = 2
 MESH = pl.DeviceIdType.MESH
 F32 = jnp.float32
@@ -80,6 +81,7 @@
     curv_ref,
     sd_ref,
     acc_ref,
+    part_ref,
     scal_ref,
     l1_ref,
     l2_ref,
@@ -94,8 +96,6 @@
     wt_ref,
     load_sem,
     small_sem,
-    l_send,
-    l_recv,
     f_send,
     f_recv,
     g_send,
@@ -118,6 +118,8 @@
     rows, cols = x_ref.shape
     half = rows // 2
     own_cols = cols // CORES
+    wide = cols // WIDE
+    loads = rows // BLOCK * WIDE
     pieces = [(sum(SUBS[:s]), SUBS[s]) for s in range(len(SUBS))]
 
     def turn(at, by):
@@ -138,8 +140,8 @@
     partner = (px * CORES + (1 - core), ft)
 
     def load(i):
-        piece = pl.ds(sum(LOAD[:i]), LOAD[i])
-        return pltpu.make_async_copy(x_hbm.at[piece], x_ref.at[piece], load_sem.at[i])
+        at = pl.ds(i // WIDE * BLOCK, BLOCK), pl.ds(i % WIDE * wide, wide)
+        return pltpu.make_async_copy(x_hbm.at[at], x_ref.at[at], load_sem.at[i])
 
     small = [
         pltpu.make_async_copy(w_hbm, d_ref, small_sem.at[0]),
@@ -160,7 +162,7 @@
         pl.semaphore_signal(barrier, inc=1, device_id=peer, device_id_type=MESH)
 
     small[0].wait()
-    for i in range(EARLY, len(LOAD)):
+    for i in range(EARLY, loads):
         load(i).start()
     wb_ref[...] = d_ref[...].astype(BF16)
     r_ref[...] = jnp.zeros_like(r_ref)
@@ -186,31 +188,35 @@
         for k in (2, 1, 3):
             send(ref.at[at], ref.at[at], send_sem, recv_sem, peer(k))
 
+    def wait_all(ref, sem):
+        pltpu.make_async_copy(ref, ref, sem).wait()
+
     def wait_group(ref, sem):
-        others = ref.at[pl.ds(0, ref.shape[0] - 1)]
-        pltpu.make_async_copy(others, others, sem).wait()
+        wait_all(ref.at[pl.ds(0, ref.shape[0] - 1)], sem)
 
     at_1, peer_1 = (py, pz), (y_peer, z_peer)
     at_2, peer_2 = (pz, py), (z_peer, y_peer)
 
-    for i in range(len(LOAD)):
-        start = sum(LOAD[:i])
-        load(i).wait()
-        h, into = divmod(start, half)
-        l1_ref[h, at_1[h], :, into : into + LOAD[i]] = dot(
-            wb_ref[...], x_ref[start : start + LOAD[i], :], 1, 1
-        )
-        if into + LOAD[i] == half:
-            if h == 0:
-                pl.semaphore_wait(barrier, len(greeted))
-            to_ring(l1_ref.at[h], at_1[h], l_send.at[0, h], l_recv.at[0, h], peer_1[h])
+    block, sent = BLOCK, 0
+    for start in range(0, rows, block):
+        at = slice(start, start + block)
+        for k in range(WIDE):
+            load(start // block * WIDE + k).wait()
+            over = slice(k * wide, (k + 1) * wide)
+            part = dot(wb_ref[:, over], x_ref[at, over], 1, 1)
+            acc_ref[:, at] = part if k == 0 else acc_ref[:, at] + part
+        if start == 0:
+            pl.semaphore_wait(barrier, len(greeted))
+        while sent < 2 and (sent + 1) * half <= start + block:
+            h, sent = sent, sent + 1
+            l1_ref[h, at_1[h]] = acc_ref[:, h * half : (h + 1) * half]
+            to_ring(l1_ref.at[h], at_1[h], f_send.at[0], f_recv.at[1, 0, h], peer_1[h])
     small[1].wait()
     small[2].wait()
     wt_ref[dp] = row_tile_sum(row_of(weights_ref, 0, rows).astype(F32))
     to_dp(wt_ref, wt_send.at[0], wt_recv.at[0])
 
     def turn_over(first, last):
-        block = 512
         per_row = cols // block
 
         def one(i, _):
@@ -227,9 +233,9 @@
 
     turn_over(0, blocks // 2)
     for h in range(2):
-        wait_group(l1_ref.at[h], l_recv.at[0, h])
+        wait_group(l1_ref.at[h], f_recv.at[1, 0, h])
         l2_ref[h, at_2[h]] = ordered_sum(l1_ref.at[h], RING)
-        to_ring(l2_ref.at[h], at_2[h], l_send.at[1, h], l_recv.at[1, h], peer_2[h])
+        to_ring(l2_ref.at[h], at_2[h], f_send.at[1], f_recv.at[1, 1, h], peer_2[h])
     turn_over(blocks // 2, blocks)
     wait_group(wt_ref, wt_recv.at[0])
     weight_total = whole_sum(ordered_sum(wt_ref, RING * CORES))
@@ -237,7 +243,7 @@
     loss_tile = None
     classes = lax.broadcasted_iota(jnp.int32, (w_hbm.shape[0], half), 0)
     for h in range(2):
-        wait_group(l2_ref.at[h], l_recv.at[1, h])
+        wait_group(l2_ref.at[h], f_recv.at[1, 1, h])
         at = slice(h * half, (h + 1) * half)
         logits = ordered_sum(l2_ref.at[h], RING)
         row_top = jnp.max(logits, axis=0, keepdims=True)
@@ -256,14 +262,13 @@
         curv_ref[:, at] = (row_scale * (class_prob - onehot)).astype(BF16)
     q_ref[0, dp] = loss_tile
     to_dp(q_ref.at[0], q_send.at[0], q_recv.at[0])
-    for h in range(2):
-        wait_group(l1_ref.at[h], l_send.at[0, h])
-        wait_group(l2_ref.at[h], l_send.at[1, h])
+    wait_all(l1_ref.at[:, pl.ds(1, RING - 1)], f_send.at[0])
+    wait_all(l2_ref.at[:, pl.ds(1, RING - 1)], f_send.at[1])
     wait_group(wt_ref, wt_send.at[0])
 
     def wait_dp(slot):
         wait_group(q_ref.at[slot], q_recv.at[slot])
-        wait_group(q_ref.at[slot], q_send.at[slot])
+        wait_group(q_ref.at[slot], q_send.at[0])
         return whole_sum(ordered_sum(q_ref.at[slot], RING * CORES))
 
     one = jnp.ones((8, 128), F32)
@@ -287,7 +292,7 @@
                 send(
                     ca_ref.at[slot, 0, :, piece],
                     ca_ref.at[slot, 1, :, piece],
-                    ca_send.at[slot, s],
+                    ca_send.at[0],
                     ca_recv.at[slot, s],
                     partner,
                 )
@@ -296,10 +301,13 @@
             start = pl.multiple_of(mine + at, 128)
             piece = pl.ds(at, size)
             part = dot(curv_ref[...], x_ref[:, pl.ds(start, size)], 1, 0)
+            part_ref[:, piece] = part
             ca_copies[s].wait_recv()
-            xs_ref[slot, px, :, piece] = (part + ca_ref[slot, 1, :, piece].astype(F32)).astype(BF16)
+            xs_ref[slot, px, :, piece] = (
+                part_ref[:, piece] + ca_ref[slot, 1, :, piece].astype(F32)
+            ).astype(BF16)
             to_ring(
-                xs_ref.at[slot, :, :, piece], px, xs_send.at[slot, s], xs_recv.at[slot, s], x_peer
+                xs_ref.at[slot, :, :, piece], px, xs_send.at[0], xs_recv.at[slot, s], x_peer
             )
 
         reduced = wait_dp(slot)
@@ -328,6 +336,12 @@
 
         tiles = []
         cb_copies = []
+
+        def take_theirs(s):
+            at, size = pieces[s]
+            cb_copies[s].wait_recv()
+            return advance(theirs + at, size, cb_ref[slot, 1, :, pl.ds(at, size)])
+
         for s, (at, size) in enumerate(pieces):
             piece = pl.ds(at, size)
             wait_group(xs_ref.at[slot, :, :, piece], xs_recv.at[slot, s])
@@ -337,7 +351,7 @@
                 send(
                     cb_ref.at[slot, 0, :, piece],
                     cb_ref.at[slot, 1, :, piece],
-                    cb_send.at[slot, s],
+                    cb_send.at[0],
                     cb_recv.at[slot, s],
                     partner,
                 )
@@ -345,45 +359,36 @@
             residual, turned = advance(mine + at, size, image)
             scores = dot(residual, turned[...], 1, 0)
             acc_ref[...] = scores if s == 0 else acc_ref[...] + scores
-        for s, (at, size) in enumerate(pieces):
-            cb_copies[s].wait_recv()
-            residual, turned = advance(theirs + at, size, cb_ref[slot, 1, :, pl.ds(at, size)])
-            if s < len(pieces) - 1:
+            if s > 0:
+                residual, turned = take_theirs(s - 1)
                 acc_ref[...] = acc_ref[...] + dot(residual, turned[...], 1, 0)
+        residual, turned = take_theirs(len(pieces) - 1)
 
         for i in range(2):
             total = tiles[0][i]
             for both in tiles[1:]:
                 total = total + both[i]
             g1_ref[slot, py, i] = total
-        to_ring(g1_ref.at[slot], py, g_send.at[slot, 0], g_recv.at[slot, 0], y_peer)
+        to_ring(g1_ref.at[slot], py, g_send.at[0], g_recv.at[slot, 0], y_peer)
+        scores = (acc_ref[...] + dot(residual, turned[...], 1, 0)).astype(BF16)
         for h in range(2):
-            at = slice(h * half, (h + 1) * half)
-            f1_ref[slot, h, at_1[h]] = (acc_ref[:, at] + dot(residual, turned[:, at], 1, 0)).astype(
-                BF16
-            )
-            to_ring(
-                f1_ref.at[slot, h], at_1[h], f_send.at[slot, 0, h], f_recv.at[slot, 0, h], peer_1[h]
-            )
+            f1_ref[slot, h, at_1[h]] = scores[:, h * half : (h + 1) * half]
+            to_ring(f1_ref.at[slot, h], at_1[h], f_send.at[0], f_recv.at[slot, 0, h], peer_1[h])
         wait_group(g1_ref.at[slot], g_recv.at[slot, 0])
         g2_ref[slot, pz] = ordered_sum(g1_ref.at[slot], RING)
-        to_ring(g2_ref.at[slot], pz, g_send.at[slot, 1], g_recv.at[slot, 1], z_peer)
+        to_ring(g2_ref.at[slot], pz, g_send.at[1], g_recv.at[slot, 1], z_peer)
         for h in range(2):
             wait_group(f1_ref.at[slot, h], f_recv.at[slot, 0, h])
             f2_ref[slot, h, at_2[h]] = ordered_sum(f1_ref.at[slot, h], RING).astype(BF16)
-            to_ring(
-                f2_ref.at[slot, h], at_2[h], f_send.at[slot, 1, h], f_recv.at[slot, 1, h], peer_2[h]
-            )
-        for s, (at, size) in enumerate(pieces):
-            wait_group(xs_ref.at[slot, :, :, pl.ds(at, size)], xs_send.at[slot, s])
-        for copy in ca_copies + cb_copies:
-            copy.wait_send()
-        for h in range(2):
-            wait_group(f1_ref.at[slot, h], f_send.at[slot, 0, h])
-        wait_group(g1_ref.at[slot], g_send.at[slot, 0])
+            to_ring(f2_ref.at[slot, h], at_2[h], f_send.at[1], f_recv.at[slot, 1, h], peer_2[h])
+        wait_group(xs_ref.at[slot], xs_send.at[0])
+        wait_all(ca_ref.at[slot, 0], ca_send.at[0])
+        wait_all(cb_ref.at[slot, 0], cb_send.at[0])
+        wait_all(f1_ref.at[slot, :, pl.ds(1, RING - 1)], f_send.at[0])
+        wait_group(g1_ref.at[slot], g_send.at[0])
 
         wait_group(g2_ref.at[slot], g_recv.at[slot, 1])
-        wait_group(g2_ref.at[slot], g_send.at[slot, 1])
+        wait_group(g2_ref.at[slot], g_send.at[1])
         sums = ordered_sum(g2_ref.at[slot], RING)
         new_norm = whole_sum(sums[0])
         cross = whole_sum(sums[1])
@@ -405,9 +410,8 @@
             part = tile_sum(scores * curv.astype(F32))
             curvature = part if curvature is None else curvature + part
         q_ref[1 - slot, dp] = curvature
-        to_dp(q_ref.at[1 - slot], q_send.at[1 - slot], q_recv.at[1 - slot])
-        for h in range(2):
-            wait_group(f2_ref.at[slot, h], f_send.at[slot, 1, h])
+        to_dp(q_ref.at[1 - slot], q_send.at[0], q_recv.at[1 - slot])
+        wait_all(f2_ref.at[slot, :, pl.ds(1, RING - 1)], f_send.at[1])
         return 0
 
     lax.fori_loop(0, CG_ITERS, iteration, 0)
@@ -450,6 +454,7 @@
             pltpu.VMEM((classes, rows), BF16),
             pltpu.VMEM((classes, rows), F32),
             pltpu.VMEM((classes, rows), F32),
+            pltpu.VMEM((classes, own_cols), F32),
             pltpu.VMEM((3, 8, 128), F32),
             pltpu.VMEM((2, RING, classes, half), F32),
             pltpu.VMEM((2, RING, classes, half), F32),
@@ -462,21 +467,19 @@
             pltpu.VMEM((2, RING, classes, own_cols), BF16),
             pltpu.VMEM((2, RING * CORES, 8, 128), F32),
             pltpu.VMEM((RING * CORES, 8, 128), F32),
-            dma((len(LOAD),)),
+            dma((rows // BLOCK * WIDE,)),
             dma((4,)),
+            dma((2,)),
+            dma((2, 2, 2)),
+            dma((2,)),
             dma((2, 2)),
-            dma((2, 2)),
-            dma((2, 2, 2)),
-            dma((2, 2, 2)),
-            dma((2, 2)),
-            dma((2, 2)),
+            dma((1,)),
             dma((2, subs)),
+            dma((1,)),
             dma((2, subs)),
+            dma((1,)),
             dma((2, subs)),
-            dma((2, subs)),
-            dma((2, subs)),
-            dma((2, subs)),
-            dma((2,)),
+            dma((1,)),
             dma((2,)),
             dma((1,)),
             dma((1,)),

time: 93.6 us -> 91.7 us (0.980)
  Pallas kernels: 89.5 us -> 87.7 us
    pallas_call x1, Pallas kernels: 89.5 us -> 87.7 us  [on_device(): pl.pallas_call(kernel, out_shape=(jax.ShapeDtypeStruct((classes, rows), F...]
where the time goes in v3:
time: 91.7 us; the launch traced here: 90.6 us
  Pallas kernels  87.7 us (96%)
  between operations  2.33 us (3%)
    pallas_call x1, Pallas kernels, on_device(): pl.pallas_call(kernel, out_shape=(jax.ShapeDtypeStruct((classes, rows), F...  87.7 us

profile of v3, /device:TPU:0, one launch (start us, length us, event | category | flops | bytes accessed | tf_op | source)
XLA Modules:
  0.0 90.6 jit_solution(15529809620599341007)
XLA Ops:
  0.6 87.7 %newton_cg.1 = (f32[16,1536]{1,0:T(8,128)S(1)}, f32[1,1]{1,0:T(1,128)}) custom-call(bf16[1536,4096]{1,0:T(8,128)(2,1)} %x_hbm.1, f32[16,4096]{1,0:T(8,128)} %w_hbm.1, s32[1536]{0:T(1024)} %labels_hbm.1, s32[1536]{0:T(1024)} %weights_hbm.1), custom_call_target="tpu_custom_call" | custom-call | tf_op jit(solution)/shard_map/newton_cg/pallas_call | solution.py:435
  88.3 0.6 copy.8

commit v4 on v3

--- a/solution.py
+++ b/solution.py
@@ -13,7 +13,7 @@
 
 RING = 4
 CORES = 2
-SUBS = (512, 1024, 512)
+SUBS = (512, 768, 768)
 BLOCK = 512
 WIDE = 2
 EARLY = 2

time: 91.7 us -> 91 us (level)
  no operation moved by 1% of the time
where the time goes in v4:
time: 91 us; the launch traced here: 89.9 us
  Pallas kernels  87 us (96%)
  between operations  2.33 us (3%)
    pallas_call x1, Pallas kernels, on_device(): pl.pallas_call(kernel, out_shape=(jax.ShapeDtypeStruct((classes, rows), F...  87 us

profile of v4, /device:TPU:0, one launch (start us, length us, event | category | flops | bytes accessed | tf_op | source)
XLA Modules:
  0.0 89.9 jit_solution(5424285983291608721)
XLA Ops:
  0.6 87.0 %newton_cg.1 = (f32[16,1536]{1,0:T(8,128)S(1)}, f32[1,1]{1,0:T(1,128)}) custom-call(bf16[1536,4096]{1,0:T(8,128)(2,1)} %x_hbm.1, f32[16,4096]{1,0:T(8,128)} %w_hbm.1, s32[1536]{0:T(1024)} %labels_hbm.1, s32[1536]{0:T(1024)} %weights_hbm.1), custom_call_target="tpu_custom_call" | custom-call | tf_op jit(solution)/shard_map/newton_cg/pallas_call | solution.py:435
  87.6 0.6 copy.8
